TPU v7x, 32 devices: a whole 2x2x4 slice. The times are simulated.
32 devices in a mesh: blk: 8 (over z, y), rep: 4 (over x, core).
Axes of the slice: x: 2, y: 2, z: 4, core: 2. Of those that a mesh axis runs over, the one named last changes fastest.
Arguments:
- resident_keys: int32 [16384], P('blk'), may hold values from 0 to 4095
- moving_keys: int32 [65536], P(('blk', 'rep')), may hold values from 0 to 4095
- payload: float32 [65536, 128], P(('blk', 'rep')), may hold values from -6 to 6
Outputs:
- joined: float32 [16384, 128], P(('blk', 'rep'))
All inputs are finite; a program needn't handle non-finite values.
Results may differ from a plain program's by a relative error of at most 0.0003.
Values sent between devices are 32-bit elements; how exact they have to be, the bound alone decides.
A program may use at most 64 MiB of HBM per device.

v0:
```python
import jax
import jax.numpy as jnp
from jax import lax
from jax.sharding import PartitionSpec as P

REACH = 2


def from_behind(block, axis, distance):
    devices = range(lax.axis_size(axis))
    route = [((i - distance) % len(devices), i) for i in devices]
    return lax.ppermute(block, axis, route)


def match_rows(res_keys, mov_keys, mov_pay):
    count = res_keys.shape[0]
    block = min(512, count)
    grouped = res_keys.reshape(count // block, block)

    def one_block(keys_here):
        hot = (keys_here[:, None] == mov_keys[None, :]).astype(jnp.float32)
        return jnp.dot(
            hot, mov_pay, precision=lax.Precision.HIGHEST, preferred_element_type=jnp.float32
        )

    return lax.map(one_block, grouped).reshape(count, mov_pay.shape[1])


def local(resident_keys, moving_keys, payload):
    total = match_rows(resident_keys, moving_keys, payload)
    for distance in range(1, REACH + 1):
        upward = from_behind((moving_keys, payload), "blk", distance)
        total = total + match_rows(resident_keys, upward[0], upward[1])
        downward = from_behind((moving_keys, payload), "blk", -distance)
        total = total + match_rows(resident_keys, downward[0], downward[1])
    return lax.psum_scatter(total, "rep", scatter_dimension=0, tiled=True)


def solution(mesh):
    in_specs = (P("blk"), P(("blk", "rep")), P(("blk", "rep"), None))
    out_specs = P(("blk", "rep"), None)
    return jax.shard_map(local, mesh=mesh, in_specs=in_specs, out_specs=out_specs, check_vma=False)
```

profile of v0, /device:TPU:0, one launch (start us, length us, event | category | flops | bytes accessed | tf_op | source)
XLA Modules:
  0.0 145.7 jit_solution(10789618133341168161)
XLA Ops:
  6.5 3.0 %collective-permute-start.1 = (f32[2048,128]{1,0:T(8,128)}, f32[2048,128]{1,0:T(8,128)S(1)}, u32[]{:S(2)}, u32[]{:S(2)}) collective-permute-start(f32[2048,128]{1,0:T(8,128)} %param.15), channel_id=1, source_target_pairs={{28,0},{0,4},{4,8},{8,12},{12,16},{16,20},{20,24},{24,28},{29,1},{... | collective-permute-start | bytes 3145736 | tf_op jit(solution)/shard_map/ppermute | solution.py:12
  9.5 3.0 %collective-permute-start.3 = (f32[2048,128]{1,0:T(8,128)}, f32[2048,128]{1,0:T(8,128)}, u32[]{:S(2)}, u32[]{:S(2)}) collective-permute-start(f32[2048,128]{1,0:T(8,128)} %param.15), channel_id=1, source_target_pairs={{4,0},{8,4},{12,8},{16,12},{20,16},{24,20},{28,24},{0,28},{5,1},{9... | collective-permute-start | bytes 3145736 | tf_op jit(solution)/shard_map/ppermute | solution.py:12
  12.6 0.0 collective-permute-start
  12.6 4.7 %collective-permute-start.2 = (s32[2048]{0:T(1024)}, s32[2048]{0:T(1024)S(1)}, u32[]{:S(2)}, u32[]{:S(2)}) collective-permute-start(s32[2048]{0:T(1024)} %param.14), channel_id=1, source_target_pairs={{4,0},{8,4},{12,8},{16,12},{20,16},{24,20},{28,24},{0,28},{5,1},{9... | collective-permute-start | bytes 24584 | tf_op jit(solution)/shard_map/ppermute | solution.py:12
  17.3 0.0 collective-permute-start.5
  17.3 0.7 reshape.31
  18.0 0.1 broadcast.8.clone.3
  18.1 12.9 %while.50 = (s32[]{:T(128)}, f32[4,512,128]{2,1,0:T(8,128)S(1)}, s32[4,512]{1,0:T(4,128)S(1)}, s32[2048]{0:T(1024)S(1)}, f32[2048,128]{1,0:T(8,128)}, /*index=5*/s32[]{:T(128)}) while((s32[]{:T(128)}, f32[4,512,128]{2,1,0:T(8,128)S(1)}, s32[4,512]{1,0:T(4,128)S(1)}, s32[2048]{0:T(1024)S(1)}, f32[2048,128]{1,0:T(8,128)}, ...), condition=%wide.region_1.2_spmd, body=%wide.region_0.1_spmd.sunk | while | flops 1611661312 | bytes 1325133 | solution.py:26
  18.1 3.2 %fusion.72 = f32[4,512,128]{2,1,0:T(8,128)S(1)} fusion(f32[4,512,128]{2,1,0:T(8,128)S(1)} %get-tuple-element.411, s32[]{:T(128)} %get-tuple-element.410, f32[2048,128]{1,0:T(8,128)} %get-tuple-element.420, s32[2048]{0:T(1024)S(1)} %get-tuple-element.419, s32[512]{0:T(512)S(1)} %bitcast.62), kind=kOutput, calls=%fused_computation.5.clone.1 | convolution fusion | flops 1611661312 | bytes 1320964 | tf_op jit(solution)/shard_map/while/body/eval_jaxpr/dot_general | solution.py:22
  21.4 3.2 %fusion.72 = f32[4,512,128]{2,1,0:T(8,128)S(1)} fusion(f32[4,512,128]{2,1,0:T(8,128)S(1)} %get-tuple-element.411, s32[]{:T(128)} %get-tuple-element.410, f32[2048,128]{1,0:T(8,128)} %get-tuple-element.420, s32[2048]{0:T(1024)S(1)} %get-tuple-element.419, s32[512]{0:T(512)S(1)} %bitcast.62), kind=kOutput, calls=%fused_computation.5.clone.1 | convolution fusion | flops 1611661312 | bytes 1320964 | tf_op jit(solution)/shard_map/while/body/eval_jaxpr/dot_general | solution.py:22
  24.6 3.2 %fusion.72 = f32[4,512,128]{2,1,0:T(8,128)S(1)} fusion(f32[4,512,128]{2,1,0:T(8,128)S(1)} %get-tuple-element.411, s32[]{:T(128)} %get-tuple-element.410, f32[2048,128]{1,0:T(8,128)} %get-tuple-element.420, s32[2048]{0:T(1024)S(1)} %get-tuple-element.419, s32[512]{0:T(512)S(1)} %bitcast.62), kind=kOutput, calls=%fused_computation.5.clone.1 | convolution fusion | flops 1611661312 | bytes 1320964 | tf_op jit(solution)/shard_map/while/body/eval_jaxpr/dot_general | solution.py:22
  27.8 3.2 %fusion.72 = f32[4,512,128]{2,1,0:T(8,128)S(1)} fusion(f32[4,512,128]{2,1,0:T(8,128)S(1)} %get-tuple-element.411, s32[]{:T(128)} %get-tuple-element.410, f32[2048,128]{1,0:T(8,128)} %get-tuple-element.420, s32[2048]{0:T(1024)S(1)} %get-tuple-element.419, s32[512]{0:T(512)S(1)} %bitcast.62), kind=kOutput, calls=%fused_computation.5.clone.1 | convolution fusion | flops 1611661312 | bytes 1320964 | tf_op jit(solution)/shard_map/while/body/eval_jaxpr/dot_general | solution.py:22
  31.0 24.0 %collective-permute-done = s32[2048]{0:T(1024)S(1)} collective-permute-done((s32[2048]{0:T(1024)}, s32[2048]{0:T(1024)S(1)}, u32[]{:S(2)}, u32[]{:S(2)}) %collective-permute-start) | collective-permute-done | bytes 8224 | tf_op jit(solution)/shard_map/ppermute | solution.py:12
  55.0 1.6 %collective-permute-start.4 = (s32[2048]{0:T(1024)S(1)}, s32[2048]{0:T(1024)S(1)}, u32[]{:S(2)}, u32[]{:S(2)}) collective-permute-start(s32[2048]{0:T(1024)S(1)} %get-tuple-element.451), channel_id=1, source_target_pairs={{24,0},{28,4},{0,8},{4,12},{8,16},{12,20},{16,24},{20,28},{25,1},{... | collective-permute-start | bytes 24584 | tf_op jit(solution)/shard_map/ppermute | solution.py:12
  56.6 0.0 collective-permute-done.1
  56.6 2.2 %collective-permute-start.7 = (f32[2048,128]{1,0:T(8,128)}, f32[2048,128]{1,0:T(8,128)}, u32[]{:S(2)}, u32[]{:S(2)}) collective-permute-start(f32[2048,128]{1,0:T(8,128)} %param.15), channel_id=1, source_target_pairs={{8,0},{12,4},{16,8},{20,12},{24,16},{28,20},{0,24},{4,28},{9,1},{1... | collective-permute-start | bytes 3145736 | tf_op jit(solution)/shard_map/ppermute | solution.py:12
  58.8 0.1 broadcast.8.clone.4
  58.9 8.0 %while.51 = (s32[]{:T(128)}, f32[4,512,128]{2,1,0:T(8,128)S(1)}, s32[4,512]{1,0:T(4,128)S(1)}, s32[2048]{0:T(1024)S(1)}, f32[2048,128]{1,0:T(8,128)S(1)}, /*index=5*/s32[]{:T(128)}) while((s32[]{:T(128)}, f32[4,512,128]{2,1,0:T(8,128)S(1)}, s32[4,512]{1,0:T(4,128)S(1)}, s32[2048]{0:T(1024)S(1)}, f32[2048,128]{1,0:T(8,128)S(1)}, ...), condition=%wide.region_3.4_spmd, body=%wide.region_2.3_spmd.sunk | while | flops 1611661312 | bytes 1325133 | solution.py:26
  58.9 2.0 %fusion.75 = f32[4,512,128]{2,1,0:T(8,128)S(1)} fusion(f32[4,512,128]{2,1,0:T(8,128)S(1)} %get-tuple-element.429, s32[]{:T(128)} %get-tuple-element.428, f32[2048,128]{1,0:T(8,128)S(1)} %get-tuple-element.438, s32[2048]{0:T(1024)S(1)} %get-tuple-element.437, s32[512]{0:T(512)S(1)} %bitcast.63), kind=kOutput, calls=%fused_computation.12.clone.1 | convolution fusion | flops 1611661312 | bytes 1320964 | tf_op jit(solution)/shard_map/while/body/eval_jaxpr/dot_general | solution.py:22
  60.9 2.0 %fusion.75 = f32[4,512,128]{2,1,0:T(8,128)S(1)} fusion(f32[4,512,128]{2,1,0:T(8,128)S(1)} %get-tuple-element.429, s32[]{:T(128)} %get-tuple-element.428, f32[2048,128]{1,0:T(8,128)S(1)} %get-tuple-element.438, s32[2048]{0:T(1024)S(1)} %get-tuple-element.437, s32[512]{0:T(512)S(1)} %bitcast.63), kind=kOutput, calls=%fused_computation.12.clone.1 | convolution fusion | flops 1611661312 | bytes 1320964 | tf_op jit(solution)/shard_map/while/body/eval_jaxpr/dot_general | solution.py:22
  63.0 2.0 %fusion.75 = f32[4,512,128]{2,1,0:T(8,128)S(1)} fusion(f32[4,512,128]{2,1,0:T(8,128)S(1)} %get-tuple-element.429, s32[]{:T(128)} %get-tuple-element.428, f32[2048,128]{1,0:T(8,128)S(1)} %get-tuple-element.438, s32[2048]{0:T(1024)S(1)} %get-tuple-element.437, s32[512]{0:T(512)S(1)} %bitcast.63), kind=kOutput, calls=%fused_computation.12.clone.1 | convolution fusion | flops 1611661312 | bytes 1320964 | tf_op jit(solution)/shard_map/while/body/eval_jaxpr/dot_general | solution.py:22
  65.0 2.0 %fusion.75 = f32[4,512,128]{2,1,0:T(8,128)S(1)} fusion(f32[4,512,128]{2,1,0:T(8,128)S(1)} %get-tuple-element.429, s32[]{:T(128)} %get-tuple-element.428, f32[2048,128]{1,0:T(8,128)S(1)} %get-tuple-element.438, s32[2048]{0:T(1024)S(1)} %get-tuple-element.437, s32[512]{0:T(512)S(1)} %bitcast.63), kind=kOutput, calls=%fused_computation.12.clone.1 | convolution fusion | flops 1611661312 | bytes 1320964 | tf_op jit(solution)/shard_map/while/body/eval_jaxpr/dot_general | solution.py:22
  67.0 1.9 %collective-permute-start.6 = (s32[2048]{0:T(1024)S(1)}, s32[2048]{0:T(1024)S(1)}, u32[]{:S(2)}, u32[]{:S(2)}) collective-permute-start(s32[2048]{0:T(1024)S(1)} %get-tuple-element.451), channel_id=1, source_target_pairs={{8,0},{12,4},{16,8},{20,12},{24,16},{28,20},{0,24},{4,28},{9,1},{1... | collective-permute-start | bytes 24584 | tf_op jit(solution)/shard_map/ppermute | solution.py:12
  68.8 0.1 broadcast.8.clone.2
  68.9 12.9 %while.52 = (s32[]{:T(128)}, f32[4,512,128]{2,1,0:T(8,128)S(1)}, s32[4,512]{1,0:T(4,128)S(1)}, s32[2048]{0:T(1024)S(1)}, f32[2048,128]{1,0:T(8,128)}, /*index=5*/s32[]{:T(128)}) while((s32[]{:T(128)}, f32[4,512,128]{2,1,0:T(8,128)S(1)}, s32[4,512]{1,0:T(4,128)S(1)}, s32[2048]{0:T(1024)S(1)}, f32[2048,128]{1,0:T(8,128)}, ...), condition=%wide.region_5.6_spmd, body=%wide.region_4.5_spmd.sunk | while | flops 1611661312 | bytes 1325133 | solution.py:26
  68.9 3.2 %fusion.78 = f32[4,512,128]{2,1,0:T(8,128)S(1)} fusion(f32[4,512,128]{2,1,0:T(8,128)S(1)} %get-tuple-element.393, s32[]{:T(128)} %get-tuple-element.392, f32[2048,128]{1,0:T(8,128)} %get-tuple-element.402, s32[2048]{0:T(1024)S(1)} %get-tuple-element.401, s32[512]{0:T(512)S(1)} %bitcast.64), kind=kOutput, calls=%fused_computation.19.clone.1 | convolution fusion | flops 1611661312 | bytes 1320964 | tf_op jit(solution)/shard_map/while/body/eval_jaxpr/dot_general | solution.py:22
  72.2 3.2 %fusion.78 = f32[4,512,128]{2,1,0:T(8,128)S(1)} fusion(f32[4,512,128]{2,1,0:T(8,128)S(1)} %get-tuple-element.393, s32[]{:T(128)} %get-tuple-element.392, f32[2048,128]{1,0:T(8,128)} %get-tuple-element.402, s32[2048]{0:T(1024)S(1)} %get-tuple-element.401, s32[512]{0:T(512)S(1)} %bitcast.64), kind=kOutput, calls=%fused_computation.19.clone.1 | convolution fusion | flops 1611661312 | bytes 1320964 | tf_op jit(solution)/shard_map/while/body/eval_jaxpr/dot_general | solution.py:22
  75.4 3.2 %fusion.78 = f32[4,512,128]{2,1,0:T(8,128)S(1)} fusion(f32[4,512,128]{2,1,0:T(8,128)S(1)} %get-tuple-element.393, s32[]{:T(128)} %get-tuple-element.392, f32[2048,128]{1,0:T(8,128)} %get-tuple-element.402, s32[2048]{0:T(1024)S(1)} %get-tuple-element.401, s32[512]{0:T(512)S(1)} %bitcast.64), kind=kOutput, calls=%fused_computation.19.clone.1 | convolution fusion | flops 1611661312 | bytes 1320964 | tf_op jit(solution)/shard_map/while/body/eval_jaxpr/dot_general | solution.py:22
  78.6 3.2 %fusion.78 = f32[4,512,128]{2,1,0:T(8,128)S(1)} fusion(f32[4,512,128]{2,1,0:T(8,128)S(1)} %get-tuple-element.393, s32[]{:T(128)} %get-tuple-element.392, f32[2048,128]{1,0:T(8,128)} %get-tuple-element.402, s32[2048]{0:T(1024)S(1)} %get-tuple-element.401, s32[512]{0:T(512)S(1)} %bitcast.64), kind=kOutput, calls=%fused_computation.19.clone.1 | convolution fusion | flops 1611661312 | bytes 1320964 | tf_op jit(solution)/shard_map/while/body/eval_jaxpr/dot_general | solution.py:22
  81.9 0.0 collective-permute-done.4
  81.9 0.0 collective-permute-done.5
  81.9 1.2 broadcast.8.clone.1
  83.0 0.1 copy-done
  83.2 15.6 %while.53 = (s32[]{:T(128)}, f32[4,512,128]{2,1,0:T(8,128)}, s32[4,512]{1,0:T(4,128)S(1)}, s32[2048]{0:T(1024)S(1)}, f32[2048,128]{1,0:T(8,128)}, /*index=5*/s32[]{:T(128)}) while((s32[]{:T(128)}, f32[4,512,128]{2,1,0:T(8,128)}, s32[4,512]{1,0:T(4,128)S(1)}, s32[2048]{0:T(1024)S(1)}, f32[2048,128]{1,0:T(8,128)}, /*index=5*/s32[]{:T(128)}) %tuple.89), condition=%wide.region_7.8_spmd, body=%wide.region_6.7_spmd.sunk | while | flops 1611661312 | bytes 1325641 | solution.py:26
  83.2 3.9 %fusion.81 = f32[4,512,128]{2,1,0:T(8,128)} fusion(f32[4,512,128]{2,1,0:T(8,128)} %get-tuple-element.375, s32[]{:T(128)} %get-tuple-element.374, f32[2048,128]{1,0:T(8,128)} %get-tuple-element.384, s32[2048]{0:T(1024)S(1)} %get-tuple-element.383, s32[512]{0:T(512)S(1)} %bitcast.65), kind=kOutput, calls=%fused_computation.26.clone.1 | convolution fusion | flops 1611661312 | bytes 1321472 | tf_op jit(solution)/shard_map/while/body/eval_jaxpr/dot_general | solution.py:22
  87.1 3.9 %fusion.81 = f32[4,512,128]{2,1,0:T(8,128)} fusion(f32[4,512,128]{2,1,0:T(8,128)} %get-tuple-element.375, s32[]{:T(128)} %get-tuple-element.374, f32[2048,128]{1,0:T(8,128)} %get-tuple-element.384, s32[2048]{0:T(1024)S(1)} %get-tuple-element.383, s32[512]{0:T(512)S(1)} %bitcast.65), kind=kOutput, calls=%fused_computation.26.clone.1 | convolution fusion | flops 1611661312 | bytes 1321472 | tf_op jit(solution)/shard_map/while/body/eval_jaxpr/dot_general | solution.py:22
  91.0 3.9 %fusion.81 = f32[4,512,128]{2,1,0:T(8,128)} fusion(f32[4,512,128]{2,1,0:T(8,128)} %get-tuple-element.375, s32[]{:T(128)} %get-tuple-element.374, f32[2048,128]{1,0:T(8,128)} %get-tuple-element.384, s32[2048]{0:T(1024)S(1)} %get-tuple-element.383, s32[512]{0:T(512)S(1)} %bitcast.65), kind=kOutput, calls=%fused_computation.26.clone.1 | convolution fusion | flops 1611661312 | bytes 1321472 | tf_op jit(solution)/shard_map/while/body/eval_jaxpr/dot_general | solution.py:22
  94.9 3.9 %fusion.81 = f32[4,512,128]{2,1,0:T(8,128)} fusion(f32[4,512,128]{2,1,0:T(8,128)} %get-tuple-element.375, s32[]{:T(128)} %get-tuple-element.374, f32[2048,128]{1,0:T(8,128)} %get-tuple-element.384, s32[2048]{0:T(1024)S(1)} %get-tuple-element.383, s32[512]{0:T(512)S(1)} %bitcast.65), kind=kOutput, calls=%fused_computation.26.clone.1 | convolution fusion | flops 1611661312 | bytes 1321472 | tf_op jit(solution)/shard_map/while/body/eval_jaxpr/dot_general | solution.py:22
  98.8 0.0 collective-permute-done.7
  98.8 0.1 broadcast.8.clone
  98.9 12.9 %while.54 = (s32[]{:T(128)}, f32[4,512,128]{2,1,0:T(8,128)S(1)}, s32[4,512]{1,0:T(4,128)S(1)}, s32[2048]{0:T(1024)S(1)}, f32[2048,128]{1,0:T(8,128)}, /*index=5*/s32[]{:T(128)}) while((s32[]{:T(128)}, f32[4,512,128]{2,1,0:T(8,128)S(1)}, s32[4,512]{1,0:T(4,128)S(1)}, s32[2048]{0:T(1024)S(1)}, f32[2048,128]{1,0:T(8,128)}, ...), condition=%wide.region_9.10_spmd, body=%wide.region_8.9_spmd.sunk | while | flops 1611661312 | bytes 1325133 | solution.py:26
  98.9 3.2 %fusion.84 = f32[4,512,128]{2,1,0:T(8,128)S(1)} fusion(f32[4,512,128]{2,1,0:T(8,128)S(1)} %get-tuple-element.357, s32[]{:T(128)} %get-tuple-element.356, f32[2048,128]{1,0:T(8,128)} %get-tuple-element.366, s32[2048]{0:T(1024)S(1)} %get-tuple-element.365, s32[512]{0:T(512)S(1)} %bitcast.66), kind=kOutput, calls=%fused_computation.33.clone.1 | convolution fusion | flops 1611661312 | bytes 1320964 | tf_op jit(solution)/shard_map/while/body/eval_jaxpr/dot_general | solution.py:22
  102.1 3.2 %fusion.84 = f32[4,512,128]{2,1,0:T(8,128)S(1)} fusion(f32[4,512,128]{2,1,0:T(8,128)S(1)} %get-tuple-element.357, s32[]{:T(128)} %get-tuple-element.356, f32[2048,128]{1,0:T(8,128)} %get-tuple-element.366, s32[2048]{0:T(1024)S(1)} %get-tuple-element.365, s32[512]{0:T(512)S(1)} %bitcast.66), kind=kOutput, calls=%fused_computation.33.clone.1 | convolution fusion | flops 1611661312 | bytes 1320964 | tf_op jit(solution)/shard_map/while/body/eval_jaxpr/dot_general | solution.py:22
  105.4 3.2 %fusion.84 = f32[4,512,128]{2,1,0:T(8,128)S(1)} fusion(f32[4,512,128]{2,1,0:T(8,128)S(1)} %get-tuple-element.357, s32[]{:T(128)} %get-tuple-element.356, f32[2048,128]{1,0:T(8,128)} %get-tuple-element.366, s32[2048]{0:T(1024)S(1)} %get-tuple-element.365, s32[512]{0:T(512)S(1)} %bitcast.66), kind=kOutput, calls=%fused_computation.33.clone.1 | convolution fusion | flops 1611661312 | bytes 1320964 | tf_op jit(solution)/shard_map/while/body/eval_jaxpr/dot_general | solution.py:22
  108.6 3.2 %fusion.84 = f32[4,512,128]{2,1,0:T(8,128)S(1)} fusion(f32[4,512,128]{2,1,0:T(8,128)S(1)} %get-tuple-element.357, s32[]{:T(128)} %get-tuple-element.356, f32[2048,128]{1,0:T(8,128)} %get-tuple-element.366, s32[2048]{0:T(1024)S(1)} %get-tuple-element.365, s32[512]{0:T(512)S(1)} %bitcast.66), kind=kOutput, calls=%fused_computation.33.clone.1 | convolution fusion | flops 1611661312 | bytes 1320964 | tf_op jit(solution)/shard_map/while/body/eval_jaxpr/dot_general | solution.py:22
  111.8 2.9 %add_add_fusion = f32[4,512,128]{2,1,0:T(8,128)} fusion(f32[4,512,128]{2,1,0:T(8,128)S(1)} %get-tuple-element.144, f32[4,512,128]{2,1,0:T(8,128)} %get-tuple-element.143, f32[4,512,128]{2,1,0:T(8,128)} %copy-done, f32[4,512,128]{2,1,0:T(8,128)S(1)} %get-tuple-element.140, f32[4,512,128]{2,1,0:T(8,128)S(1)} %get-tuple-element.141), kind=kLoop, calls=%fused_computation.35 | loop fusion | flops 1048576 | bytes 6291456 | tf_op jit(solution)/shard_map/add | solution.py:35
  114.7 0.0 reduce-scatter.2.cloned.1.call-update
  114.7 24.1 %reduce-scatter.2.cloned.1.call-done = f32[512,128]{1,0:T(8,128)} async-done(((f32[2048,128]{1,0:T(8,128)}), f32[512,128]{1,0:T(8,128)}) %reduce-scatter.2.cloned.1.call-update) | async-done | bytes 262160 | tf_op jit(solution)/shard_map/reduce_scatter | solution.py:36
  (27 shorter events, 0.2 us)
Async XLA Ops:
  6.5 11.5 %copy-start.1 = (s32[2048]{0:T(1024)S(1)}, s32[2048]{0:T(1024)}, u32[]{:S(2)}) copy-start(s32[2048]{0:T(1024)} %param.14) | copy-start | bytes 24580
  6.5 132.3 %reduce-scatter.2.cloned.1.call-start = ((), (), s32[]{:S(2)}) async-start(), calls=%async_computation.1 | async-start | bytes 1310720 | tf_op jit(solution)/shard_map/reduce_scatter | solution.py:36
  6.5 50.0 %collective-permute-start.1 = (f32[2048,128]{1,0:T(8,128)}, f32[2048,128]{1,0:T(8,128)S(1)}, u32[]{:S(2)}, u32[]{:S(2)}) collective-permute-start(f32[2048,128]{1,0:T(8,128)} %param.15), channel_id=1, source_target_pairs={{28,0},{0,4},{4,8},{8,12},{12,16},{16,20},{20,24},{24,28},{29,1},{... | collective-permute-start | bytes 3145736 | tf_op jit(solution)/shard_map/ppermute | solution.py:12
  9.5 59.3 %collective-permute-start.3 = (f32[2048,128]{1,0:T(8,128)}, f32[2048,128]{1,0:T(8,128)}, u32[]{:S(2)}, u32[]{:S(2)}) collective-permute-start(f32[2048,128]{1,0:T(8,128)} %param.15), channel_id=1, source_target_pairs={{4,0},{8,4},{12,8},{16,12},{20,16},{24,20},{28,24},{0,28},{5,1},{9... | collective-permute-start | bytes 3145736 | tf_op jit(solution)/shard_map/ppermute | solution.py:12
  12.6 42.4 %collective-permute-start = (s32[2048]{0:T(1024)}, s32[2048]{0:T(1024)S(1)}, u32[]{:S(2)}, u32[]{:S(2)}) collective-permute-start(s32[2048]{0:T(1024)} %param.14), channel_id=1, source_target_pairs={{28,0},{0,4},{4,8},{8,12},{12,16},{16,20},{20,24},{24,28},{29,1},{... | collective-permute-start | bytes 24584 | tf_op jit(solution)/shard_map/ppermute | solution.py:12
  12.6 54.4 %collective-permute-start.2 = (s32[2048]{0:T(1024)}, s32[2048]{0:T(1024)S(1)}, u32[]{:S(2)}, u32[]{:S(2)}) collective-permute-start(s32[2048]{0:T(1024)} %param.14), channel_id=1, source_target_pairs={{4,0},{8,4},{12,8},{16,12},{20,16},{24,20},{28,24},{0,28},{5,1},{9... | collective-permute-start | bytes 24584 | tf_op jit(solution)/shard_map/ppermute | solution.py:12
  17.3 64.6 %collective-permute-start.5 = (f32[2048,128]{1,0:T(8,128)}, f32[2048,128]{1,0:T(8,128)}, u32[]{:S(2)}, u32[]{:S(2)}) collective-permute-start(f32[2048,128]{1,0:T(8,128)} %param.15), channel_id=1, source_target_pairs={{24,0},{28,4},{0,8},{4,12},{8,16},{12,20},{16,24},{20,28},{25,1},{... | collective-permute-start | bytes 3145736 | tf_op jit(solution)/shard_map/ppermute | solution.py:12
  55.0 26.9 %collective-permute-start.4 = (s32[2048]{0:T(1024)S(1)}, s32[2048]{0:T(1024)S(1)}, u32[]{:S(2)}, u32[]{:S(2)}) collective-permute-start(s32[2048]{0:T(1024)S(1)} %get-tuple-element.451), channel_id=1, source_target_pairs={{24,0},{28,4},{0,8},{4,12},{8,16},{12,20},{16,24},{20,28},{25,1},{... | collective-permute-start | bytes 24584 | tf_op jit(solution)/shard_map/ppermute | solution.py:12
  56.6 42.2 %collective-permute-start.7 = (f32[2048,128]{1,0:T(8,128)}, f32[2048,128]{1,0:T(8,128)}, u32[]{:S(2)}, u32[]{:S(2)}) collective-permute-start(f32[2048,128]{1,0:T(8,128)} %param.15), channel_id=1, source_target_pairs={{8,0},{12,4},{16,8},{20,12},{24,16},{28,20},{0,24},{4,28},{9,1},{1... | collective-permute-start | bytes 3145736 | tf_op jit(solution)/shard_map/ppermute | solution.py:12
  67.0 31.8 %collective-permute-start.6 = (s32[2048]{0:T(1024)S(1)}, s32[2048]{0:T(1024)S(1)}, u32[]{:S(2)}, u32[]{:S(2)}) collective-permute-start(s32[2048]{0:T(1024)S(1)} %get-tuple-element.451), channel_id=1, source_target_pairs={{8,0},{12,4},{16,8},{20,12},{24,16},{28,20},{0,24},{4,28},{9,1},{1... | collective-permute-start | bytes 24584 | tf_op jit(solution)/shard_map/ppermute | solution.py:12
  81.8 1.3 copy-start
Sparse Core Ops, SparseCore 0:
  114.9 23.9 reduce-scatter.1
where the time goes:
time: 146 us
  matrix products  61.9 us (42%)
  waiting for transfers between devices  48.1 us (33%)
  starting transfers between devices  16.4 us (11%)
  between operations  13.5 us (9%)
  other arithmetic  2.9 us (2%)
  local copies, waits for them, and re-layouts  2.43 us (2%)
    dot_general x20, matrix products, one_block(): jnp.dot(hot, mov_pay, precision=lax.Precision.HIGHEST, preferred_element_...  61.9 us
    reduce_scatter x1, waiting for transfers between devices, local(): return lax.psum_scatter(total, 'rep', scatter_dimension=0, tiled=True)  24.1 us
    ppermute x8, waiting for transfers between devices, from_behind(): return lax.ppermute(block, axis, route)  24 us
    ppermute x8, starting transfers between devices, from_behind(): return lax.ppermute(block, axis, route)  16.4 us
  transfers between devices with their start and end apart: 9, of which 2 were waited for; matrix products, arithmetic and copies ran while one was open for 35% of the time, Pallas kernels for 0%

commit v1 on v0

v1 whole, which is shorter than its diff:
```python
import functools

import jax
import jax.numpy as jnp
from jax import lax
from jax.experimental import pallas as pl
from jax.experimental.pallas import tpu as pltpu
from jax.sharding import PartitionSpec as P

REACH = 2
LANES = 128
CHUNK = 512


def kernel(
    n_blk, groups, rk_ref, mk_ref, pay_ref, out_ref,
    other_pay, mkeys, rkeys, hl, kcol, acc, abuf, xrecv, bbuf, sbuf, brecv,
    key_send, key_recv, pair_send, pair_recv, x_send, x_recv, b_send, b_recv,
):
    blk = lax.axis_index("blk")
    rep = lax.axis_index("rep")
    group, core = rep // 2, rep % 2
    rows = pay_ref.shape[0]
    width = pay_ref.shape[1]
    quarter = out_ref.shape[0]
    key_rows = mk_ref.shape[0]
    qrows = quarter // LANES
    par = blk % 2 if n_blk % 2 == 0 else 0
    near = 2 * par - 1
    offs = [REACH, -REACH, near, -near]
    key_to = [-REACH, REACH] + ([near, -near] if n_blk % 2 == 0 else [-near, near])
    slots = len(offs)

    def at(off):
        return lax.rem(blk + off + n_blk, n_blk)

    mate = rep + 1 - 2 * core
    peers = [lax.rem(group + d, groups) * 2 + core for d in range(1, groups)]

    barrier = pltpu.get_barrier_semaphore()
    pl.semaphore_signal(barrier, inc=1, device_id={"rep": mate})
    for p in peers:
        pl.semaphore_signal(barrier, inc=1, device_id={"rep": p})
    for o in offs:
        pl.semaphore_signal(barrier, inc=1, device_id={"blk": at(o)})
    mkeys[0:key_rows] = mk_ref[...]
    rkeys[slots] = rk_ref[...]
    pl.semaphore_wait(barrier, 1 + len(peers) + slots)

    sends = []
    pays = []
    pair_keys = pltpu.make_async_remote_copy(
        src_ref=mk_ref, dst_ref=mkeys.at[pl.ds(key_rows, key_rows)],
        send_sem=pair_send.at[0], recv_sem=pair_recv.at[0], device_id={"rep": mate})
    pair_keys.start()
    pair_pay = pltpu.make_async_remote_copy(
        src_ref=pay_ref, dst_ref=other_pay,
        send_sem=pair_send.at[1], recv_sem=pair_recv.at[1], device_id={"rep": mate})
    pair_pay.start()
    keys = []
    for i in range(slots):
        c = pltpu.make_async_remote_copy(
            src_ref=rk_ref, dst_ref=rkeys.at[i],
            send_sem=key_send.at[i], recv_sem=key_recv.at[i],
            device_id={"blk": at(key_to[i])})
        c.start()
        keys.append(c)

    def split(src, base):
        @pl.loop(0, rows // CHUNK)
        def _(k):
            v = src[pl.ds(k * CHUNK, CHUNK), :]
            hi = v.astype(jnp.bfloat16)
            lo = (v - hi.astype(jnp.float32)).astype(jnp.bfloat16)
            hl[pl.ds(base + k * CHUNK, CHUNK), 0:width] = hi
            hl[pl.ds(base + k * CHUNK, CHUNK), width:2 * width] = lo

    split(pay_ref, 0)
    pair_keys.wait_recv()
    pair_pay.wait_recv()
    split(other_pay, rows)

    def partial(slot, q, dst):
        for j in range(qrows):
            row = rkeys[slot, pl.ds(q * qrows + j, 1), :]
            kcol[j * LANES:(j + 1) * LANES, :] = jnp.broadcast_to(row, (LANES, LANES)).T
        acc[...] = jnp.zeros_like(acc)
        per = CHUNK // LANES

        @pl.loop(0, 2 * rows // CHUNK)
        def _(k):
            mine = kcol[...]
            hot = []
            for g in range(per):
                row = mkeys[pl.ds(k * per + g, 1), :]
                hot.append(jnp.where(mine == row, 1.0, 0.0).astype(jnp.bfloat16))
            hot = jnp.concatenate(hot, axis=1)
            acc[...] += jnp.dot(hot, hl[pl.ds(k * CHUNK, CHUNK), :],
                                preferred_element_type=jnp.float32)

        dst[...] = acc[:, 0:width] + acc[:, width:2 * width]

    x_copies = []
    b_copies = []

    def finish(i):
        total = bbuf[i]
        for d in range(groups - 1):
            x_copies[i][d].wait_recv()
            total = total + xrecv[i, d]
        if i == slots:
            return total
        sbuf[i] = total
        c = pltpu.make_async_remote_copy(
            src_ref=sbuf.at[i], dst_ref=brecv.at[i],
            send_sem=b_send.at[i], recv_sem=b_recv.at[i],
            device_id={"blk": at(offs[i])})
        c.start()
        b_copies.append(c)

    for i in range(slots + 1):
        if i < slots:
            keys[i].wait_recv()
        x_copies.append([])
        for d, p in enumerate(peers):
            partial(i, p, abuf.at[i, d])
            c = pltpu.make_async_remote_copy(
                src_ref=abuf.at[i, d], dst_ref=xrecv.at[i, d],
                send_sem=x_send.at[i, d], recv_sem=x_recv.at[i, d],
                device_id={"rep": p})
            c.start()
            x_copies[i].append(c)
        partial(i, rep, bbuf.at[i])
        if i >= 1:
            finish(i - 1)
    total = finish(slots)
    for i in range(slots):
        b_copies[i].wait_recv()
        total = total + brecv[i]
    out_ref[...] = total
    pair_keys.wait_send()
    pair_pay.wait_send()
    for c in keys + b_copies:
        c.wait_send()
    for row in x_copies:
        for c in row:
            c.wait_send()


def solution(mesh):
    n_blk, n_rep = mesh.shape["blk"], mesh.shape["rep"]
    groups = n_rep // 2
    slots = 4

    def local(resident_keys, moving_keys, payload):
        res, rows, width = resident_keys.shape[0], payload.shape[0], payload.shape[1]
        quarter = res // n_rep
        f32, bf16, i32 = jnp.float32, jnp.bfloat16, jnp.int32
        vmem = pl.BlockSpec(memory_space=pltpu.VMEM)
        dma = pltpu.SemaphoreType.DMA
        return pl.pallas_call(
            functools.partial(kernel, n_blk, groups),
            out_shape=jax.ShapeDtypeStruct((quarter, width), f32),
            in_specs=[vmem, vmem, vmem],
            out_specs=vmem,
            scratch_shapes=[
                pltpu.VMEM((rows, width), f32),
                pltpu.VMEM((2 * rows // LANES, LANES), i32),
                pltpu.VMEM((slots + 1, res // LANES, LANES), i32),
                pltpu.VMEM((2 * rows, 2 * width), bf16),
                pltpu.VMEM((quarter, LANES), i32),
                pltpu.VMEM((quarter, 2 * width), f32),
                pltpu.VMEM((slots + 1, groups - 1, quarter, width), f32),
                pltpu.VMEM((slots + 1, groups - 1, quarter, width), f32),
                pltpu.VMEM((slots + 1, quarter, width), f32),
                pltpu.VMEM((slots, quarter, width), f32),
                pltpu.VMEM((slots, quarter, width), f32),
                dma((slots,)), dma((slots,)),
                dma((2,)), dma((2,)),
                dma((slots + 1, groups - 1)), dma((slots + 1, groups - 1)),
                dma((slots,)), dma((slots,)),
            ],
            compiler_params=pltpu.CompilerParams(
                collective_id=0, has_side_effects=True, vmem_limit_bytes=48 * 1024 * 1024),
        )(resident_keys.reshape(res // LANES, LANES), moving_keys.reshape(rows // LANES, LANES), payload)

    in_specs = (P("blk"), P(("blk", "rep")), P(("blk", "rep"), None))
    out_specs = P(("blk", "rep"), None)
    return jax.shard_map(local, mesh=mesh, in_specs=in_specs, out_specs=out_specs, check_vma=False)
```

time: 146 us -> 48 us (0.33)
  matrix products: 61.9 us -> 0 us
  waiting for transfers between devices: 48.1 us -> 0 us
  Pallas kernels: 0 us -> 44.3 us
  starting transfers between devices: 16.4 us -> 0 us
  between operations: 13.5 us -> 0.01 us
  other arithmetic: 2.9 us -> 0 us
    dot_general x20 -> x0, matrix products: 61.9 us -> none  [one_block(): jnp.dot(hot, mov_pay, precision=lax.Precision.HIGHEST, preferred_element_...]
    pallas_call x0 -> x1, Pallas kernels: none -> 44.3 us  [local(): pl.pallas_call(functools.partial(kernel, n_blk, groups), out_shape=jax.Sh...]
    reduce_scatter x1 -> x0, waiting for transfers between devices: 24.1 us -> none  [local(): return lax.psum_scatter(total, 'rep', scatter_dimension=0, tiled=True)]
    ppermute x8 -> x0, waiting for transfers between devices: 24 us -> none  [from_behind(): return lax.ppermute(block, axis, route)]
    ppermute x8 -> x0, starting transfers between devices: 16.4 us -> none  [from_behind(): return lax.ppermute(block, axis, route)]
    unnamed x4 -> x7, local copies, waits for them, and re-layouts: 0.15 us -> 3.32 us
    add x1 -> x0, other arithmetic: 2.9 us -> none  [local(): total = total + match_rows(resident_keys, downward[0], downward[1])]
  transfers between devices with their start and end apart: 9 -> 0, of which waited for: 2 -> 0; matrix products, arithmetic and copies ran while one was open for 35% -> 0% of each run, Pallas kernels for 0% -> 0%
where the time goes in v1:
time: 48 us; the launch traced here: 47.7 us
  Pallas kernels  44.3 us (92%)
  local copies, waits for them, and re-layouts  3.32 us (7%)
    pallas_call x1, Pallas kernels, local(): pl.pallas_call(functools.partial(kernel, n_blk, groups), out_shape=jax.Sh...  44.3 us
    unnamed x7, local copies, waits for them, and re-layouts  3.32 us

profile of v1, /device:TPU:0, one launch (start us, length us, event | category | flops | bytes accessed | tf_op | source)
XLA Modules:
  0.0 47.7 jit_solution(11947311174492701799)
XLA Ops:
  0.0 0.0 copy-start
  0.0 1.2 %copy-done = f32[2048,128]{1,0:T(8,128)S(1)} copy-done((f32[2048,128]{1,0:T(8,128)S(1)}, f32[2048,128]{1,0:T(8,128)}, u32[]{:S(2)}) %copy-start) | copy-done | bytes 1048600
  1.2 0.0 copy-start.1
  1.2 0.7 %copy-done.1 = s32[2048]{0:T(1024)S(1)} copy-done((s32[2048]{0:T(1024)S(1)}, s32[2048]{0:T(1024)}, u32[]{:S(2)}) %copy-start.1) | copy-done | bytes 8216
  1.9 0.0 copy-start.2
  1.9 0.7 %copy-done.2 = s32[2048]{0:T(1024)S(1)} copy-done((s32[2048]{0:T(1024)S(1)}, s32[2048]{0:T(1024)}, u32[]{:S(2)}) %copy-start.2) | copy-done | bytes 8216
  2.6 44.3 %shard_map.37 = f32[512,128]{1,0:T(8,128)S(1)} custom-call(s32[16,128]{1,0:T(8,128)S(1)} %bitcast.2, s32[16,128]{1,0:T(8,128)S(1)} %bitcast.3, f32[2048,128]{1,0:T(8,128)S(1)} %copy-done), custom_call_target="tpu_custom_call" | custom-call | tf_op jit(solution)/shard_map/pallas_call | solution.py:161
  47.0 0.7 %copy.5 = f32[512,128]{1,0:T(8,128)} copy(f32[512,128]{1,0:T(8,128)S(1)} %shard_map.37) | data formatting | bytes 524288
Async XLA Ops:
  0.0 1.2 %copy-start = (f32[2048,128]{1,0:T(8,128)S(1)}, f32[2048,128]{1,0:T(8,128)}, u32[]{:S(2)}) copy-start(f32[2048,128]{1,0:T(8,128)} %pay_ref.1) | copy-start | bytes 3145732
  1.2 0.7 %copy-start.1 = (s32[2048]{0:T(1024)S(1)}, s32[2048]{0:T(1024)}, u32[]{:S(2)}) copy-start(s32[2048]{0:T(1024)} %param.3) | copy-start | bytes 24580
  1.9 0.7 %copy-start.2 = (s32[2048]{0:T(1024)S(1)}, s32[2048]{0:T(1024)}, u32[]{:S(2)}) copy-start(s32[2048]{0:T(1024)} %param.4) | copy-start | bytes 24580

commit v2 on v1

v2 whole, which is shorter than its diff:
```python
import functools

import jax
import jax.numpy as jnp
from jax import lax
from jax.experimental import pallas as pl
from jax.experimental.pallas import tpu as pltpu
from jax.sharding import PartitionSpec as P

REACH = 2
LANES = 128
CHUNK = 2048


def kernel(
    n_blk, groups, rk_ref, mk_ref, pay_ref, out_ref,
    pay, other_pay, mkeys, rkeys, hl, kcol, abuf, xrecv, bbuf, sbuf, brecv, yrecv,
    in_sem, key_send, key_recv, pair_send, pair_recv, x_send, x_recv, b_send, b_recv, y_send, y_recv,
):
    blk = lax.axis_index("blk")
    rep = lax.axis_index("rep")
    group, core = rep // 2, rep % 2
    rows, width = pay.shape
    quarter = out_ref.shape[0]
    key_rows = mk_ref.shape[0]
    qrows = quarter // LANES
    fold = n_blk % 2 == 0
    near = 2 * (blk % 2) - 1 if fold else -1
    offs = [REACH, -REACH, near, -near]
    key_to = [-REACH, REACH] + ([near, -near] if fold else [-near, near])
    own = len(offs)

    def at(off):
        return lax.rem(blk + off + n_blk, n_blk)

    mate = rep + 1 - 2 * core
    peers = [lax.rem(group + d, groups) * 2 + core for d in range(1, groups)]

    load_pay = pltpu.make_async_copy(pay_ref, pay, in_sem.at[0])
    load_mk = pltpu.make_async_copy(mk_ref, mkeys.at[pl.ds(0, key_rows)], in_sem.at[1])
    load_rk = pltpu.make_async_copy(rk_ref, rkeys.at[own], in_sem.at[2])
    for c in (load_pay, load_mk, load_rk):
        c.start()

    barrier = pltpu.get_barrier_semaphore()
    for o in offs:
        pl.semaphore_signal(barrier, inc=1, device_id={"blk": at(o)})
    for p in peers + [mate]:
        pl.semaphore_signal(barrier, inc=1, device_id={"rep": p})
    pl.semaphore_wait(barrier, 1 + len(peers) + own)

    sent = []

    def send(src, dst, send_sem, recv_sem, to):
        c = pltpu.make_async_remote_copy(
            src_ref=src, dst_ref=dst, send_sem=send_sem, recv_sem=recv_sem, device_id=to)
        c.start()
        sent.append(c)
        return c

    keys = {}
    for i in (0, 3, 2, 1):
        keys[i] = send(rk_ref, rkeys.at[i], key_send.at[i], key_recv.at[i], {"blk": at(key_to[i])})
    pair_keys = send(mk_ref, mkeys.at[pl.ds(key_rows, key_rows)], pair_send.at[0], pair_recv.at[0], {"rep": mate})
    pair_pay = send(pay_ref, other_pay, pair_send.at[1], pair_recv.at[1], {"rep": mate})

    def split(src, base):
        @pl.loop(0, rows // 256)
        def _(k):
            v = src[pl.ds(k * 256, 256), :]
            hi = v.astype(jnp.bfloat16)
            lo = (v - hi.astype(jnp.float32)).astype(jnp.bfloat16)
            hl[pl.ds(base + k * 256, 256), 0:width] = hi
            hl[pl.ds(base + k * 256, 256), width:2 * width] = lo

    for c in (load_pay, load_mk, load_rk):
        c.wait()
    split(pay, 0)
    pair_keys.wait_recv()
    pair_pay.wait_recv()
    split(other_pay, rows)

    per = CHUNK // LANES

    def partial(slot, q):
        for j in range(qrows):
            row = rkeys[slot, pl.ds(q * qrows + j, 1), :]
            kcol[j * LANES:(j + 1) * LANES, :] = jnp.broadcast_to(row, (LANES, LANES)).T

        def part(k):
            mine = kcol[...]
            hot = []
            for g in range(per):
                row = mkeys[pl.ds(k * per + g, 1), :]
                hot.append(jnp.where(mine == row, 1.0, 0.0).astype(jnp.bfloat16))
            both = jnp.dot(jnp.concatenate(hot, axis=1), hl[pl.ds(k * CHUNK, CHUNK), :],
                           preferred_element_type=jnp.float32)
            return both[:, 0:width] + both[:, width:2 * width]

        return part, 2 * rows // CHUNK

    def compute(slot, q, dst):
        part, steps = partial(slot, q)
        if steps == 1:
            dst[...] = part(0)
            return
        dst[...] = part(0)

        @pl.loop(1, steps)
        def _(k):
            dst[...] += part(k)

    waiting = {}

    def send_x(i):
        waiting[i] = [
            send(abuf.at[i, d], xrecv.at[i, d], x_send.at[i, d], x_recv.at[i, d], {"rep": p})
            for d, p in enumerate(peers)]

    ready = set()

    def for_peers(i):
        if i != own and i not in ready:
            keys[i].wait_recv()
            ready.add(i)
        for d, p in enumerate(peers):
            compute(i, p, abuf.at[i, d])

    def for_me(i):
        compute(i, rep, bbuf.at[i])

    def finish(i):
        total = bbuf[i]
        for d, c in enumerate(waiting[i]):
            c.wait_recv()
            total = total + xrecv[i, d]
        return total

    def give(i):
        sbuf[i] = finish(i)
        return send(sbuf.at[i], brecv.at[i], b_send.at[i], b_recv.at[i], {"blk": at(offs[i])})

    def give_partner(src, d):
        return send(src, yrecv.at[d], y_send.at[d], y_recv.at[d], {"blk": at(offs[3])})

    for_peers(0)
    send_x(0)
    for_peers(3)
    if fold:
        folded = [give_partner(abuf.at[3, d], d) for d in range(groups - 1)]
    else:
        send_x(3)
    for_me(0)
    for_peers(2)
    send_x(2)
    given = [give(0)]
    for_peers(1)
    send_x(1)
    for_me(3)
    if fold:
        last = give_partner(bbuf.at[3], groups - 1)
    for_me(2)
    for_peers(own)
    if fold:
        for d, c in enumerate(folded):
            c.wait_recv()
            abuf[own, d] = abuf[own, d] + yrecv[d]
    send_x(own)
    given.append(give(2))
    for_me(1)
    if not fold:
        given.append(give(3))
    for_me(own)
    given.append(give(1))
    total = bbuf[own]
    if fold:
        last.wait_recv()
        total = total + yrecv[groups - 1]
    bbuf[own] = total
    total = finish(own)
    for i, c in zip((0, 2, 1) if fold else (0, 2, 3, 1), given):
        c.wait_recv()
        total = total + brecv[i]
    out_ref[...] = total
    for c in sent:
        c.wait_send()


def solution(mesh):
    n_blk, n_rep = mesh.shape["blk"], mesh.shape["rep"]
    groups = n_rep // 2
    slots = 4

    def local(resident_keys, moving_keys, payload):
        res, rows, width = resident_keys.shape[0], payload.shape[0], payload.shape[1]
        quarter = res // n_rep
        f32, bf16, i32 = jnp.float32, jnp.bfloat16, jnp.int32
        vmem = pl.BlockSpec(memory_space=pltpu.VMEM)
        dma = pltpu.SemaphoreType.DMA
        return pl.pallas_call(
            functools.partial(kernel, n_blk, groups),
            out_shape=jax.ShapeDtypeStruct((quarter, width), f32),
            in_specs=[pl.BlockSpec(memory_space=pl.ANY)] * 3,
            out_specs=vmem,
            scratch_shapes=[
                pltpu.VMEM((rows, width), f32),
                pltpu.VMEM((rows, width), f32),
                pltpu.VMEM((2 * rows // LANES, LANES), i32),
                pltpu.VMEM((slots + 1, res // LANES, LANES), i32),
                pltpu.VMEM((2 * rows, 2 * width), bf16),
                pltpu.VMEM((quarter, LANES), i32),
                pltpu.VMEM((slots + 1, groups - 1, quarter, width), f32),
                pltpu.VMEM((slots + 1, groups - 1, quarter, width), f32),
                pltpu.VMEM((slots + 1, quarter, width), f32),
                pltpu.VMEM((slots, quarter, width), f32),
                pltpu.VMEM((slots, quarter, width), f32),
                pltpu.VMEM((groups, quarter, width), f32),
                dma((3,)),
                dma((slots,)), dma((slots,)),
                dma((2,)), dma((2,)),
                dma((slots + 1, groups - 1)), dma((slots + 1, groups - 1)),
                dma((slots,)), dma((slots,)),
                dma((groups,)), dma((groups,)),
            ],
            compiler_params=pltpu.CompilerParams(
                collective_id=0, has_side_effects=True, vmem_limit_bytes=48 * 1024 * 1024),
        )(resident_keys.reshape(res // LANES, LANES), moving_keys.reshape(rows // LANES, LANES), payload)

    in_specs = (P("blk"), P(("blk", "rep")), P(("blk", "rep"), None))
    out_specs = P(("blk", "rep"), None)
    return jax.shard_map(local, mesh=mesh, in_specs=in_specs, out_specs=out_specs, check_vma=False)
```

time: 48 us -> 40.5 us (0.84)
  Pallas kernels: 44.3 us -> 36.9 us
    pallas_call x1, Pallas kernels: 44.3 us -> 36.9 us  [local(): pl.pallas_call(functools.partial(kernel, n_blk, groups), out_shape=jax.Sh...]
where the time goes in v2:
time: 40.5 us; the launch traced here: 40.2 us
  Pallas kernels  36.9 us (91%)
  local copies, waits for them, and re-layouts  3.32 us (8%)
    pallas_call x1, Pallas kernels, local(): pl.pallas_call(functools.partial(kernel, n_blk, groups), out_shape=jax.Sh...  36.9 us
    unnamed x7, local copies, waits for them, and re-layouts  3.32 us

profile of v2, /device:TPU:0, one launch (start us, length us, event | category | flops | bytes accessed | tf_op | source)
XLA Modules:
  0.0 40.2 jit_solution(7525331939811307429)
XLA Ops:
  0.0 0.0 copy-start
  0.0 1.2 %copy-done = f32[2048,128]{1,0:T(8,128)S(1)} copy-done((f32[2048,128]{1,0:T(8,128)S(1)}, f32[2048,128]{1,0:T(8,128)}, u32[]{:S(2)}) %copy-start) | copy-done | bytes 1048600
  1.2 0.0 copy-start.1
  1.2 0.7 %copy-done.1 = s32[2048]{0:T(1024)S(1)} copy-done((s32[2048]{0:T(1024)S(1)}, s32[2048]{0:T(1024)}, u32[]{:S(2)}) %copy-start.1) | copy-done | bytes 8216
  1.9 0.0 copy-start.2
  1.9 0.7 %copy-done.2 = s32[2048]{0:T(1024)S(1)} copy-done((s32[2048]{0:T(1024)S(1)}, s32[2048]{0:T(1024)}, u32[]{:S(2)}) %copy-start.2) | copy-done | bytes 8216
  2.6 36.9 %shard_map.37 = f32[512,128]{1,0:T(8,128)S(1)} custom-call(s32[16,128]{1,0:T(8,128)S(1)} %bitcast.2, s32[16,128]{1,0:T(8,128)S(1)} %bitcast.3, f32[2048,128]{1,0:T(8,128)S(1)} %copy-done), custom_call_target="tpu_custom_call" | custom-call | tf_op jit(solution)/shard_map/pallas_call | solution.py:200
  39.5 0.7 %copy.5 = f32[512,128]{1,0:T(8,128)} copy(f32[512,128]{1,0:T(8,128)S(1)} %shard_map.37) | data formatting | bytes 524288
Async XLA Ops:
  0.0 1.2 %copy-start = (f32[2048,128]{1,0:T(8,128)S(1)}, f32[2048,128]{1,0:T(8,128)}, u32[]{:S(2)}) copy-start(f32[2048,128]{1,0:T(8,128)} %pay_ref.1) | copy-start | bytes 3145732
  1.2 0.7 %copy-start.1 = (s32[2048]{0:T(1024)S(1)}, s32[2048]{0:T(1024)}, u32[]{:S(2)}) copy-start(s32[2048]{0:T(1024)} %param.3) | copy-start | bytes 24580
  1.9 0.7 %copy-start.2 = (s32[2048]{0:T(1024)S(1)}, s32[2048]{0:T(1024)}, u32[]{:S(2)}) copy-start(s32[2048]{0:T(1024)} %param.4) | copy-start | bytes 24580

commit v3 on v2

--- a/solution.py
+++ b/solution.py
@@ -47,23 +47,6 @@
         pl.semaphore_signal(barrier, inc=1, device_id={"blk": at(o)})
     for p in peers + [mate]:
         pl.semaphore_signal(barrier, inc=1, device_id={"rep": p})
-    pl.semaphore_wait(barrier, 1 + len(peers) + own)
-
-    sent = []
-
-    def send(src, dst, send_sem, recv_sem, to):
-        c = pltpu.make_async_remote_copy(
-            src_ref=src, dst_ref=dst, send_sem=send_sem, recv_sem=recv_sem, device_id=to)
-        c.start()
-        sent.append(c)
-        return c
-
-    keys = {}
-    for i in (0, 3, 2, 1):
-        keys[i] = send(rk_ref, rkeys.at[i], key_send.at[i], key_recv.at[i], {"blk": at(key_to[i])})
-    pair_keys = send(mk_ref, mkeys.at[pl.ds(key_rows, key_rows)], pair_send.at[0], pair_recv.at[0], {"rep": mate})
-    pair_pay = send(pay_ref, other_pay, pair_send.at[1], pair_recv.at[1], {"rep": mate})
-
     def split(src, base):
         @pl.loop(0, rows // 256)
         def _(k):
@@ -76,9 +59,22 @@
     for c in (load_pay, load_mk, load_rk):
         c.wait()
     split(pay, 0)
-    pair_keys.wait_recv()
-    pair_pay.wait_recv()
-    split(other_pay, rows)
+    pl.semaphore_wait(barrier, 1 + len(peers) + own)
+
+    sent = []
+
+    def send(src, dst, send_sem, recv_sem, to):
+        c = pltpu.make_async_remote_copy(
+            src_ref=src, dst_ref=dst, send_sem=send_sem, recv_sem=recv_sem, device_id=to)
+        c.start()
+        sent.append(c)
+        return c
+
+    keys = {}
+    for i in (0, 3, 2, 1):
+        keys[i] = send(rk_ref, rkeys.at[i], key_send.at[i], key_recv.at[i], {"blk": at(key_to[i])})
+    pair_keys = send(mk_ref, mkeys.at[pl.ds(key_rows, key_rows)], pair_send.at[0], pair_recv.at[0], {"rep": mate})
+    pair_pay = send(pay_ref, other_pay, pair_send.at[1], pair_recv.at[1], {"rep": mate})
 
     per = CHUNK // LANES
 
@@ -97,18 +93,21 @@
                            preferred_element_type=jnp.float32)
             return both[:, 0:width] + both[:, width:2 * width]
 
-        return part, 2 * rows // CHUNK
-
-    def compute(slot, q, dst):
-        part, steps = partial(slot, q)
-        if steps == 1:
+        return part
+
+    def compute(slot, q, dst, first=0, last=2 * rows // CHUNK):
+        part = partial(slot, q)
+        if first == 0:
             dst[...] = part(0)
-            return
-        dst[...] = part(0)
-
-        @pl.loop(1, steps)
+
+        @pl.loop(max(first, 1), last)
         def _(k):
             dst[...] += part(k)
+
+    compute(own, rep, bbuf.at[own], last=rows // CHUNK)
+    pair_keys.wait_recv()
+    pair_pay.wait_recv()
+    split(other_pay, rows)
 
     waiting = {}
 
@@ -170,7 +169,7 @@
     for_me(1)
     if not fold:
         given.append(give(3))
-    for_me(own)
+    compute(own, rep, bbuf.at[own], first=rows // CHUNK)
     given.append(give(1))
     total = bbuf[own]
     if fold:

time: 40.5 us -> 40.5 us (level)
  no operation moved by 1% of the time
where the time goes in v3:
time: 40.5 us; the launch traced here: 40.2 us
  Pallas kernels  36.9 us (91%)
  local copies, waits for them, and re-layouts  3.32 us (8%)
    pallas_call x1, Pallas kernels, local(): pl.pallas_call(functools.partial(kernel, n_blk, groups), out_shape=jax.Sh...  36.9 us
    unnamed x7, local copies, waits for them, and re-layouts  3.32 us

profile of v3, /device:TPU:0, one launch (start us, length us, event | category | flops | bytes accessed | tf_op | source)
XLA Modules:
  0.0 40.2 jit_solution(16735438472168303690)
XLA Ops:
  0.0 0.0 copy-start
  0.0 1.2 %copy-done = f32[2048,128]{1,0:T(8,128)S(1)} copy-done((f32[2048,128]{1,0:T(8,128)S(1)}, f32[2048,128]{1,0:T(8,128)}, u32[]{:S(2)}) %copy-start) | copy-done | bytes 1048600
  1.2 0.0 copy-start.1
  1.2 0.7 %copy-done.1 = s32[2048]{0:T(1024)S(1)} copy-done((s32[2048]{0:T(1024)S(1)}, s32[2048]{0:T(1024)}, u32[]{:S(2)}) %copy-start.1) | copy-done | bytes 8216
  1.9 0.0 copy-start.2
  1.9 0.7 %copy-done.2 = s32[2048]{0:T(1024)S(1)} copy-done((s32[2048]{0:T(1024)S(1)}, s32[2048]{0:T(1024)}, u32[]{:S(2)}) %copy-start.2) | copy-done | bytes 8216
  2.6 36.9 %shard_map.37 = f32[512,128]{1,0:T(8,128)S(1)} custom-call(s32[16,128]{1,0:T(8,128)S(1)} %bitcast.2, s32[16,128]{1,0:T(8,128)S(1)} %bitcast.3, f32[2048,128]{1,0:T(8,128)S(1)} %copy-done), custom_call_target="tpu_custom_call" | custom-call | tf_op jit(solution)/shard_map/pallas_call | solution.py:199
  39.5 0.7 %copy.5 = f32[512,128]{1,0:T(8,128)} copy(f32[512,128]{1,0:T(8,128)S(1)} %shard_map.37) | data formatting | bytes 524288
Async XLA Ops:
  0.0 1.2 %copy-start = (f32[2048,128]{1,0:T(8,128)S(1)}, f32[2048,128]{1,0:T(8,128)}, u32[]{:S(2)}) copy-start(f32[2048,128]{1,0:T(8,128)} %pay_ref.1) | copy-start | bytes 3145732
  1.2 0.7 %copy-start.1 = (s32[2048]{0:T(1024)S(1)}, s32[2048]{0:T(1024)}, u32[]{:S(2)}) copy-start(s32[2048]{0:T(1024)} %param.3) | copy-start | bytes 24580
  1.9 0.7 %copy-start.2 = (s32[2048]{0:T(1024)S(1)}, s32[2048]{0:T(1024)}, u32[]{:S(2)}) copy-start(s32[2048]{0:T(1024)} %param.4) | copy-start | bytes 24580
